TPU v7x, 512 devices: a whole 4x4x16 slice. The times are simulated.
512 devices in a mesh: expert: 32 (over x, y, core), tensor: 16 (over z).
Axes of the slice: x: 4, y: 4, z: 16, core: 2. Of those that a mesh axis runs over, the one named last changes fastest.
Arguments:
- tokens: bfloat16 [1024, 7168], P('expert', 'tensor'), may hold values from -6 to 6
- expert_ids: int32 [1024, 8], P('expert'), may hold values from 0 to 31, all different within a row; in each aligned block of 32 rows (0 to 31, 32 to 63, ...) at most 24 rows name the same one
- combine: float32 [1024, 8], P('expert'), may hold values from 0.1 to 0.5
- w_in: bfloat16 [32, 7168, 2048], P('expert', None, 'tensor'), may hold values from -0.0625 to 0.0625
- w_down: bfloat16 [32, 1024, 7168], P('expert', None, 'tensor'), may hold values from -0.1875 to 0.1875
Outputs:
- moe_out: bfloat16 [1024, 7168], P('expert', 'tensor')
Inputs may be any that keep to these rules, and one draw needn't show every extreme that they name: `expert_ids`: each row names 8 different experts. Within the 32 tokens of one index of expert, no expert is named by more than 24 rows.
All inputs are finite; a program needn't handle non-finite values.
Results may differ from a plain program's by a relative error of at most 0.008.
Values may be sent and summed in bfloat16 or wider, within the bound.
No kernel may reach another device: no remote copies, remote signals or barrier semaphores. Data moves between devices by JAX's collectives and lax.ppermute only.
A program may use at most 64 MiB of HBM per device.

v0:
```python
import jax
import jax.numpy as jnp
from jax import lax
from jax.sharding import PartitionSpec as P

TOP = 8


def route_slots(expert_ids, experts):
    one_hot = (
        expert_ids[:, :, None] == jnp.arange(experts, dtype=jnp.int32)[None, None, :]
    ).astype(jnp.int32)
    per_token = jnp.sum(one_hot, axis=1)
    before = jnp.cumsum(per_token, axis=0) - per_token
    return jnp.take_along_axis(before, expert_ids, axis=1)


def per_device(tokens, expert_ids, combine, w_in, w_down):
    experts = lax.axis_size("expert")
    tok_group = tokens.shape[0]
    capacity = min(tok_group, 3 * tok_group * TOP // experts)
    slot_index = route_slots(expert_ids, experts)
    target = (expert_ids * capacity + slot_index).reshape(-1)
    w_local = w_in[0]
    down_local = w_down[0]
    feat_width = tokens.shape[1]
    spread = jnp.repeat(tokens, TOP, axis=0)
    buffer = jnp.zeros((experts * capacity, feat_width), tokens.dtype).at[target].set(spread)
    arrived = lax.all_to_all(
        buffer.reshape(experts, capacity, feat_width),
        "expert",
        split_axis=0,
        concat_axis=0,
        tiled=True,
    )
    token_rows = arrived.reshape(experts * capacity, tokens.shape[1])
    weights = w_local
    gate_up = jnp.dot(
        lax.all_gather(token_rows, "tensor", axis=1, tiled=True),
        weights,
        preferred_element_type=jnp.float32,
    )
    half_width = w_local.shape[1] // 2
    hidden = (jax.nn.silu(gate_up[:, :half_width]) * gate_up[:, half_width:]).astype(jnp.bfloat16)
    weights = down_local
    expert_out = jnp.dot(
        lax.all_gather(hidden, "tensor", axis=1, tiled=True),
        weights,
        preferred_element_type=jnp.float32,
    ).astype(jnp.bfloat16)
    returned = lax.all_to_all(
        expert_out.reshape(experts, capacity, down_local.shape[1]),
        "expert",
        split_axis=0,
        concat_axis=0,
        tiled=True,
    )
    returned_flat = returned.reshape(experts * capacity, down_local.shape[1])
    picked = returned_flat[target].reshape(tok_group, TOP, down_local.shape[1])
    combined = jnp.einsum("tk,tkd->td", combine, picked.astype(jnp.float32))
    return combined.astype(jnp.bfloat16)


def solution(mesh):
    in_specs = (
        P("expert", "tensor"),
        P("expert", None),
        P("expert", None),
        P("expert", None, "tensor"),
        P("expert", None, "tensor"),
    )
    out_specs = P("expert", "tensor")
    return jax.shard_map(
        per_device, mesh=mesh, in_specs=in_specs, out_specs=out_specs, check_vma=False
    )
```

profile of v0, /device:TPU:1, one launch (start us, length us, event | category | flops | bytes accessed | tf_op | source)
XLA Modules:
  0.0 278.9 jit_solution(17810822857758711456)
XLA Ops:
  6.5 0.0 copy-start
  6.5 0.0 all-gather.3.cloned.1.call-start
  6.5 0.9 copy.28
  7.4 0.1 convert_reduce_fusion
  7.6 0.1 reduce_window_sum.11
  7.6 0.1 reshape.75
  7.7 0.0 copy-start.1
  7.7 1.9 gather_fusion.1
  9.7 0.1 reshape.78
  9.8 0.1 reshape.60
  9.9 0.0 copy-done.1
  9.9 1.8 scatter_custom_fusion
  11.7 23.8 %all_to_all.10 = bf16[32,24,448]{2,1,0:T(8,128)(2,1)S(1)} all-to-all(bf16[32,24,448]{2,1,0:T(8,128)(2,1)S(1)} %bitcast.29), channel_id=1, replica_groups=mesh['expert'=32,'tensor'=16] {'expert'}, dimensions={0} | all-to-all | bytes 1376256 | tf_op jit(solution)/shard_map/all_to_all | solution.py:29
  35.5 1.1 copy.33
  36.6 0.0 all-gather.3.cloned.1.call-update
  36.7 0.0 copy-start.3
  36.7 0.0 all-gather.5.cloned.1.call-start
  36.7 131.4 %all-gather.3.cloned.1.call-done = bf16[768,7168]{0,1:T(8,128)(2,1)} async-done(((bf16[768,448]{0,1:T(8,128)(2,1)}), bf16[768,7168]{0,1:T(8,128)(2,1)}) %all-gather.3.cloned.1.call-update) | async-done | bytes 11010064 | tf_op jit(solution)/shard_map/all_gather | solution.py:39
  168.1 0.0 copy-done
  168.1 5.9 %fusion = f32[768,128]{0,1:T(8,128)S(1)} fusion(bf16[768,7168]{0,1:T(8,128)(2,1)} %all-gather.3.cloned.1.call-done, bf16[1,7168,128]{2,1,0:T(8,128)(2,1)S(1)} %copy-done), kind=kOutput, calls=%fused_computation.3 | convolution fusion | flops 1409286144 | bytes 13238272 | tf_op jit(solution)/shard_map/dot_general | solution.py:38
  174.0 0.7 fusion.8
  174.7 0.0 all-gather.5.cloned.1.call-update
  174.7 60.5 %all-gather.5.cloned.1.call-done = bf16[768,1024]{0,1:T(8,128)(2,1)} async-done(((bf16[768,64]{0,1:T(8,128)(2,1)}), bf16[768,1024]{0,1:T(8,128)(2,1)}) %all-gather.5.cloned.1.call-update) | async-done | bytes 1572880 | tf_op jit(solution)/shard_map/all_gather | solution.py:47
  235.2 0.0 copy-done.3
  235.2 2.3 convolution_convert_fusion
  237.5 0.0 copy-start.2
  237.5 1.2 copy.34
  238.7 17.2 %all-to-all-start.1 = ((bf16[32,24,448]{2,1,0:T(8,128)(2,1)}), bf16[32,24,448]{2,1,0:T(8,128)(2,1)S(1)}, u32[]{:S(2)}, u32[]{:S(2)}) async-start(bf16[32,24,448]{2,1,0:T(8,128)(2,1)} %bitcast.7), calls=%async_computation.1 | async-start | bytes 1572864 | tf_op jit(solution)/shard_map/all_to_all | solution.py:51
  255.9 0.0 copy-done.2
  255.9 0.1 copy.35
  256.0 14.1 %all-to-all-done.1 = bf16[32,24,448]{2,1,0:T(8,128)(2,1)S(1)} async-done(((bf16[32,24,448]{2,1,0:T(8,128)(2,1)}), bf16[32,24,448]{2,1,0:T(8,128)(2,1)S(1)}, u32[]{:S(2)}, u32[]{:S(2)}) %all-to-all-start.1) | async-done | bytes 688160 | tf_op jit(solution)/shard_map/all_to_all | solution.py:51
  270.1 1.2 gather_fusion
  271.3 0.2 fusion.5
  271.5 0.6 copy.38
  (5 shorter events, 0.0 us)
Async XLA Ops:
  6.5 161.6 %copy-start = (bf16[1,7168,128]{2,1,0:T(8,128)(2,1)S(1)}, bf16[1,7168,128]{2,1,0:T(8,128)(2,1)}, u32[]{:S(2)}) copy-start(bf16[1,7168,128]{2,1,0:T(8,128)(2,1)} %param.8) | copy-start | bytes 5505028
  6.5 161.6 %all-gather.3.cloned.1.call-start = ((), (), s32[]{:S(2)}) async-start(), calls=%async_computation.2 | async-start | bytes 11698176 | tf_op jit(solution)/shard_map/all_gather | solution.py:39
  7.7 2.2 copy-start.1
  36.7 198.5 %copy-start.3 = (bf16[1,1024,448]{1,2,0:T(8,128)(2,1)S(1)}, bf16[1,1024,448]{1,2,0:T(8,128)(2,1)}, u32[]{:S(2)}) copy-start(bf16[1,1024,448]{1,2,0:T(8,128)(2,1)} %param.9) | copy-start | bytes 2752516
  36.7 198.5 %all-gather.5.cloned.1.call-start = ((), (), s32[]{:S(2)}) async-start(), calls=%async_computation.3 | async-start | bytes 1671168 | tf_op jit(solution)/shard_map/all_gather | solution.py:47
  237.5 18.4 %copy-start.2 = (f32[32,8]{0,1:T(8,128)S(1)}, f32[32,8]{0,1:T(8,128)}, u32[]{:S(2)}) copy-start(f32[32,8]{0,1:T(8,128)} %param.7) | copy-start | bytes 3076
  238.7 31.4 %all-to-all-start.1 = ((bf16[32,24,448]{2,1,0:T(8,128)(2,1)}), bf16[32,24,448]{2,1,0:T(8,128)(2,1)S(1)}, u32[]{:S(2)}, u32[]{:S(2)}) async-start(bf16[32,24,448]{2,1,0:T(8,128)(2,1)} %bitcast.7), calls=%async_computation.1 | async-start | bytes 1572864 | tf_op jit(solution)/shard_map/all_to_all | solution.py:51
Sparse Core Ops, SparseCore 0:
  36.8 131.3 all-gather.2
  174.8 60.2 all-gather.4
where the time goes:
time: 279 us
  waiting for transfers between devices  206 us (74%)
  blocking collectives  23.8 us (9%)
  starting transfers between devices  17.3 us (6%)
  between operations  13.5 us (5%)
  local copies, waits for them, and re-layouts  9.04 us (3%)
  matrix products  8.34 us (3%)
    all_gather x1, waiting for transfers between devices, per_device(): lax.all_gather(token_rows, 'tensor', axis=1, tiled=True)  131 us
    all_gather x1, waiting for transfers between devices, per_device(): lax.all_gather(hidden, 'tensor', axis=1, tiled=True)  60.5 us
    all_to_all x1, blocking collectives, per_device(): lax.all_to_all(buffer.reshape(experts, capacity, feat_width), 'expert', s...  23.8 us
    all_to_all x1, starting transfers between devices, per_device(): lax.all_to_all(expert_out.reshape(experts, capacity, down_local.shape[1])...  17.2 us
    all_to_all x1, waiting for transfers between devices, per_device(): lax.all_to_all(expert_out.reshape(experts, capacity, down_local.shape[1])...  14.1 us
    dot_general x1, matrix products, per_device(): jnp.dot(lax.all_gather(token_rows, 'tensor', axis=1, tiled=True), weights...  5.85 us
  transfers between devices with their start and end apart: 3, of which 3 were waited for; matrix products, arithmetic and copies ran while one was open for 0% of the time, Pallas kernels for 0%

commit v1 on v0

--- a/solution.py
+++ b/solution.py
@@ -44,7 +44,9 @@
     hidden = (jax.nn.silu(gate_up[:, :half_width]) * gate_up[:, half_width:]).astype(jnp.bfloat16)
     weights = down_local
     expert_out = jnp.dot(
-        lax.all_gather(hidden, "tensor", axis=1, tiled=True),
+        jnp.concatenate(
+            lax.all_to_all(jnp.stack([hidden] * lax.axis_size("tensor")), "tensor", 0, 0), axis=1
+        ),
         weights,
         preferred_element_type=jnp.float32,
     ).astype(jnp.bfloat16)

time: 279 us -> 290 us (1.039)
  blocking collectives: 23.8 us -> 100 us
  waiting for transfers between devices: 206 us -> 146 us
  starting transfers between devices: 17.3 us -> 13.8 us
    all_to_all x0 -> x1, blocking collectives: none -> 76.6 us  [per_device(): lax.all_to_all(jnp.stack([hidden] * lax.axis_size('tensor')), 'tensor', 0...]
    all_gather x1 -> x0, waiting for transfers between devices: 60.5 us -> none  [per_device(): lax.all_gather(hidden, 'tensor', axis=1, tiled=True)]
    all_to_all x1, starting transfers between devices: 17.2 us -> 13.8 us  [per_device(): lax.all_to_all(expert_out.reshape(experts, capacity, down_local.shape[1])...]
  transfers between devices with their start and end apart: 3 -> 2, of which waited for: 3 -> 2; matrix products, arithmetic and copies ran while one was open for 0% -> 0% of each run, Pallas kernels for 0% -> 0%
where the time goes in v1:
time: 290 us
  waiting for transfers between devices  146 us (50%)
  blocking collectives  100 us (34%)
  starting transfers between devices  13.8 us (5%)
  between operations  13.5 us (5%)
  local copies, waits for them, and re-layouts  9.17 us (3%)
  matrix products  6.93 us (2%)
    all_gather x1, waiting for transfers between devices, per_device(): lax.all_gather(token_rows, 'tensor', axis=1, tiled=True)  131 us
    all_to_all x1, blocking collectives, per_device(): lax.all_to_all(jnp.stack([hidden] * lax.axis_size('tensor')), 'tensor', 0...  76.6 us
    all_to_all x1, blocking collectives, per_device(): lax.all_to_all(buffer.reshape(experts, capacity, feat_width), 'expert', s...  23.8 us
    all_to_all x1, waiting for transfers between devices, per_device(): lax.all_to_all(expert_out.reshape(experts, capacity, down_local.shape[1])...  14.1 us
    all_to_all x1, starting transfers between devices, per_device(): lax.all_to_all(expert_out.reshape(experts, capacity, down_local.shape[1])...  13.8 us
    dot_general x1, matrix products, per_device(): jnp.dot(lax.all_gather(token_rows, 'tensor', axis=1, tiled=True), weights...  5.85 us
  transfers between devices with their start and end apart: 2, of which 2 were waited for; matrix products, arithmetic and copies ran while one was open for 0% of the time, Pallas kernels for 0%

profile of v1, /device:TPU:1, one launch (start us, length us, event | category | flops | bytes accessed | tf_op | source)
XLA Modules:
  0.0 289.8 jit_solution(1957028703330903890)
XLA Ops:
  6.5 0.0 copy-start
  6.5 0.0 all-gather.2.cloned.1.call-start
  6.5 0.9 copy.29
  7.4 0.1 convert_reduce_fusion
  7.6 0.1 reduce_window_sum.11
  7.6 0.1 reshape.85
  7.7 0.0 copy-start.1
  7.7 1.9 gather_fusion.1
  9.7 0.1 reshape.88
  9.8 0.1 reshape.68
  9.9 0.0 copy-done.1
  9.9 1.8 scatter_custom_fusion
  11.7 23.8 %all_to_all.15 = bf16[32,24,448]{2,1,0:T(8,128)(2,1)S(1)} all-to-all(bf16[32,24,448]{2,1,0:T(8,128)(2,1)S(1)} %bitcast.32), channel_id=1, replica_groups=mesh['expert'=32,'tensor'=16] {'expert'}, dimensions={0} | all-to-all | bytes 1376256 | tf_op jit(solution)/shard_map/all_to_all | solution.py:29
  35.5 1.1 copy.34
  36.6 0.0 all-gather.2.cloned.1.call-update
  36.7 131.5 %all-gather.2.cloned.1.call-done = bf16[768,7168]{0,1:T(8,128)(2,1)} async-done(((bf16[768,448]{0,1:T(8,128)(2,1)}), bf16[768,7168]{0,1:T(8,128)(2,1)}) %all-gather.2.cloned.1.call-update) | async-done | bytes 11010064 | tf_op jit(solution)/shard_map/all_gather | solution.py:39
  168.1 0.0 copy-done
  168.1 5.8 %fusion = f32[768,128]{0,1:T(8,128)S(1)} fusion(bf16[768,7168]{0,1:T(8,128)(2,1)} %all-gather.2.cloned.1.call-done, bf16[1,7168,128]{2,1,0:T(8,128)(2,1)S(1)} %copy-done), kind=kOutput, calls=%fused_computation.3 | convolution fusion | flops 1409286144 | bytes 13238272 | tf_op jit(solution)/shard_map/dot_general | solution.py:38
  174.0 0.1 fusion.8
  174.1 0.1 stack.2
  174.2 0.0 copy-start.3
  174.2 76.6 %all_to_all.16 = bf16[16,768,64]{1,2,0:T(8,128)(2,1)S(1)} all-to-all(bf16[16,768,64]{1,2,0:T(8,128)(2,1)S(1)} %stack.2), channel_id=1, replica_groups=mesh['expert'=32,'tensor'=16] {'tensor'}, dimensions={0} | all-to-all | bytes 3145728 | tf_op jit(solution)/shard_map/all_to_all | solution.py:48
  250.8 0.0 copy-done.3
  250.8 0.9 convolution_convert_fusion
  251.7 0.0 copy-start.2
  251.7 1.2 copy.35
  252.9 13.8 %all-to-all-start.2 = ((bf16[32,24,448]{2,1,0:T(8,128)(2,1)}), bf16[32,24,448]{2,1,0:T(8,128)(2,1)S(1)}, u32[]{:S(2)}, u32[]{:S(2)}) async-start(bf16[32,24,448]{2,1,0:T(8,128)(2,1)} %bitcast.9), calls=%async_computation.2 | async-start | bytes 1572864 | tf_op jit(solution)/shard_map/all_to_all | solution.py:53
  266.7 0.0 copy-done.2
  266.7 0.1 copy.36
  266.8 14.1 %all-to-all-done.2 = bf16[32,24,448]{2,1,0:T(8,128)(2,1)S(1)} async-done(((bf16[32,24,448]{2,1,0:T(8,128)(2,1)}), bf16[32,24,448]{2,1,0:T(8,128)(2,1)S(1)}, u32[]{:S(2)}, u32[]{:S(2)}) %all-to-all-start.2) | async-done | bytes 688160 | tf_op jit(solution)/shard_map/all_to_all | solution.py:53
  281.0 1.2 gather_fusion
  282.1 0.2 fusion.5
  282.3 0.6 copy.39
  (5 shorter events, 0.0 us)
Async XLA Ops:
  6.5 161.6 %copy-start = (bf16[1,7168,128]{2,1,0:T(8,128)(2,1)S(1)}, bf16[1,7168,128]{2,1,0:T(8,128)(2,1)}, u32[]{:S(2)}) copy-start(bf16[1,7168,128]{2,1,0:T(8,128)(2,1)} %param.8) | copy-start | bytes 5505028
  6.5 161.6 %all-gather.2.cloned.1.call-start = ((), (), s32[]{:S(2)}) async-start(), calls=%async_computation.3 | async-start | bytes 11698176 | tf_op jit(solution)/shard_map/all_gather | solution.py:39
  7.7 2.2 copy-start.1
  174.2 76.6 %copy-start.3 = (bf16[1,1024,448]{1,2,0:T(8,128)(2,1)S(1)}, bf16[1,1024,448]{1,2,0:T(8,128)(2,1)}, u32[]{:S(2)}) copy-start(bf16[1,1024,448]{1,2,0:T(8,128)(2,1)} %param.9) | copy-start | bytes 2752516
  251.7 15.0 %copy-start.2 = (f32[32,8]{0,1:T(8,128)S(1)}, f32[32,8]{0,1:T(8,128)}, u32[]{:S(2)}) copy-start(f32[32,8]{0,1:T(8,128)} %param.7) | copy-start | bytes 3076
  252.9 28.1 %all-to-all-start.2 = ((bf16[32,24,448]{2,1,0:T(8,128)(2,1)}), bf16[32,24,448]{2,1,0:T(8,128)(2,1)S(1)}, u32[]{:S(2)}, u32[]{:S(2)}) async-start(bf16[32,24,448]{2,1,0:T(8,128)(2,1)} %bitcast.9), calls=%async_computation.2 | async-start | bytes 1572864 | tf_op jit(solution)/shard_map/all_to_all | solution.py:53
Sparse Core Ops, SparseCore 0:
  36.8 131.3 all-gather.1
